TPU v7x, 32 devices: a whole 2x2x4 slice. The times are simulated.
32 devices in a mesh: seq: 16 (over z, x, core), head: 2 (over y).
Axes of the slice: x: 2, y: 2, z: 4, core: 2. Of those that a mesh axis runs over, the one named last changes fastest.
Arguments:
- sparse_query: bfloat16 [4096, 8192], P('seq', 'head'), may hold values from -62 to 62
- sparse_key: bfloat16 [4096, 1024], P('seq', 'head'), may hold values from -5 to 5
- sparse_value: bfloat16 [4096, 1024], P('seq', 'head'), may hold values from -5 to 5
- light_query: bfloat16 [4096, 8192], P('seq', 'head'), may hold values from -60 to 60
- light_key: bfloat16 [4096, 8192], P('seq', 'head'), may hold values from -0.5 to 0.5
- log_decay: float32 [64, 4096], P('head', 'seq'), may hold values from -1 to 0
- segments: int32 [4096], P('seq'), may hold values from 0 to 3, never falling along the last dimension, each value on 1 to 2048 neighbouring positions
- block_list: int32 [32, 12], P('seq'), may hold values from -1 to 29, as said below
Outputs:
- sparse_out: bfloat16 [4096, 8192], P('seq', 'head')
- mixed_out: bfloat16 [4096, 8192], P('seq', 'head')
Inputs may be any that keep to these rules, and one draw needn't show every extreme that they name: `block_list`: entry -1 names no block. Every other entry of row b names a block of an earlier aligned group of 256 tokens than the group that holds block b; the rows of one aligned group of 256 tokens together name at most one block of any other group, and name it at most once. Some row names 12 blocks. `segments`: document ids may be packed several to a wider word wherever they travel.
All inputs are finite; a program needn't handle non-finite values.
Results may differ from a plain program's by a relative error of at most 0.0057.
Values may be sent and summed in bfloat16 or wider, within the bound.
No kernel may reach another device: no remote copies, remote signals or barrier semaphores. Data moves between devices by JAX's collectives and lax.ppermute only.
A program may use at most 128 MiB of HBM per device.

v0:
```python
import jax
import jax.numpy as jnp
from jax import lax
from jax.sharding import PartitionSpec as P

ASKER_CHANNELS = 64
HD = 128
BLK = 128
big_negative = -1e30
norm_eps = 1e-06


def passed_along(value, axis, by):
    size = lax.axis_size(axis)
    pairs = [(i, i + by) for i in range(size) if 0 <= i + by < size]
    return lax.ppermute(value, axis, pairs)


def carried_in(value, axis, join, neutral):
    count, mine = (lax.axis_size(axis), lax.axis_index(axis))
    pieces = jax.tree.map(lambda part: lax.all_gather(part, axis), value)
    subtotal = jax.tree.map(
        lambda part, zero: jnp.full_like(part, 0) + jnp.asarray(zero, part.dtype), value, neutral
    )

    def turn(position, subtotal):
        longer = join(subtotal, jax.tree.map(lambda part: part[position], pieces))
        return jax.tree.map(lambda new, old: jnp.where(position < mine, new, old), longer, subtotal)

    return lax.fori_loop(0, count - 1, turn, subtotal)


def attend_block(query, own_kv, own_seg, picked_kv, picked_seg, picked_ok):
    row_count = query.shape[0]
    kv_width = own_kv.shape[1] // 2
    kv_heads = kv_width // HD
    group_size = query.shape[1] // kv_width
    list_count = picked_kv.shape[0]
    keys_all = jnp.concatenate(
        [own_kv, picked_kv.reshape(list_count * row_count, 2 * kv_width)], axis=0
    )
    seg_all = jnp.concatenate([own_seg, picked_seg.reshape(list_count * row_count)])
    queries = query.reshape(row_count, kv_heads, group_size, HD)
    key_part = keys_all[:, :kv_width].reshape(-1, kv_heads, HD)
    value_part = keys_all[:, kv_width:].reshape(-1, kv_heads, HD)
    scores = jnp.einsum(
        "qkgd,nkd->kgqn", queries, key_part, preferred_element_type=jnp.float32
    ) * HD ** (-0.5)
    places = jnp.arange(row_count)
    causal = places[None, :] <= places[:, None]
    listed_ok = jnp.broadcast_to(
        jnp.repeat(picked_ok, row_count)[None, :], (row_count, list_count * row_count)
    )
    allowed = jnp.concatenate([causal, listed_ok], axis=1) & (seg_all[None, :] == own_seg[:, None])
    scores = jnp.where(allowed[None, None], scores, big_negative)
    highest = jnp.max(scores, axis=-1, keepdims=True)
    lifted = jnp.exp(scores - highest)
    weights = (lifted / jnp.sum(lifted, axis=-1, keepdims=True)).astype(jnp.bfloat16)
    result = jnp.einsum("kgqn,nkd->qkgd", weights, value_part, preferred_element_type=jnp.float32)
    return result.astype(jnp.bfloat16).reshape(row_count, kv_heads * group_size * HD)


def light_local(queries, keyed, valued, rates, doc_ids, prior_doc):
    running = jnp.cumsum(rates, axis=1)
    block_total = running[:, -1]
    places = jnp.arange(doc_ids.shape[0])
    spread = running[:, :, None] - running[:, None, :]
    visible = (places[None, :] <= places[:, None]) & (doc_ids[None, :] == doc_ids[:, None])
    decay_mask = jnp.where(visible[None], jnp.exp(jnp.minimum(spread, 0.0)), 0.0)
    scores = jnp.einsum("thd,shd->hts", queries, keyed, preferred_element_type=jnp.float32)
    weights = (scores * decay_mask).astype(jnp.bfloat16)
    inside = jnp.einsum("hts,shd->thd", weights, valued, preferred_element_type=jnp.float32)
    reach_factor = jnp.exp(running) * (doc_ids == prior_doc).astype(jnp.float32)[None, :]
    fading = (
        jnp.exp(block_total[:, None] - running)
        * (doc_ids == doc_ids[-1]).astype(jnp.float32)[None, :]
    )
    scaled = keyed.astype(jnp.float32) * jnp.transpose(fading)[:, :, None]
    added_state = jnp.einsum(
        "shd,she->hde", scaled, valued.astype(jnp.float32), precision=lax.Precision.HIGHEST
    )
    carry_factor = jnp.exp(block_total) * (doc_ids[-1] == prior_doc).astype(jnp.float32)
    return (inside, reach_factor, added_state, carry_factor)


def chain_link(earlier, latter):
    return (earlier[0] * latter[0], latter[0][:, None, None] * earlier[1] + latter[1])


def body(
    sparse_query, sparse_key, sparse_value, light_query, light_key, log_decay, segments, block_list
):
    tokens_here = sparse_query.shape[0]
    block_count = tokens_here // BLK
    kv_width = sparse_key.shape[1]
    shard_count = lax.axis_size("seq")
    kv_local = jnp.concatenate([sparse_key, sparse_value], axis=1)
    local_blocks = kv_local.reshape(block_count, BLK, 2 * kv_width)
    seg_blocks = segments.reshape(block_count, BLK)
    owner_index = jnp.where(block_list >= 0, block_list // block_count, -1).reshape(-1)
    inner_index = (block_list % block_count).reshape(-1)
    owner_match = jnp.arange(shard_count)[:, None] == owner_index[None, :]
    wanted = jnp.max(jnp.where(owner_match, inner_index[None, :], -1), axis=1)
    wanted_safe = jnp.clip(wanted, 0, block_count - 1)
    owner_table = owner_index.reshape(block_count, block_list.shape[1])
    kv_portion = lax.all_gather(kv_local, "seq", axis=0, tiled=True)
    seg_portion = lax.all_gather(segments, "seq", axis=0, tiled=True)
    portion_shards = kv_portion.shape[0] // tokens_here
    kv_view = kv_portion.reshape(portion_shards, block_count, BLK, 2 * kv_width)
    seg_view = seg_portion.reshape(portion_shards, block_count, BLK)
    pick_block = wanted_safe[:, None] == jnp.arange(block_count)[None, :]
    owners_here = jnp.arange(portion_shards)
    owner_hit = owner_table[:, :, None] == owners_here[None, None, :]
    selector = owner_hit[:, :, :, None] & pick_block[None, None, :, :]
    new_kv = jnp.einsum(
        "bkpj,pjnc->bknc",
        selector.astype(jnp.bfloat16),
        kv_view,
        preferred_element_type=jnp.float32,
    )
    new_seg = jnp.sum(jnp.where(selector[:, :, :, :, None], seg_view[None, None], 0), axis=(2, 3))
    picked_kv = new_kv.astype(jnp.bfloat16)
    picked_seg = new_seg.astype(jnp.int32)
    picked_ok = block_list >= 0
    query_blocks = sparse_query.reshape(block_count, BLK, sparse_query.shape[1])
    sparse_out = jnp.concatenate(
        [
            attend_block(
                query_blocks[block_index],
                local_blocks[block_index],
                seg_blocks[block_index],
                picked_kv[block_index],
                picked_seg[block_index],
                picked_ok[block_index],
            )
            for block_index in range(block_count)
        ],
        axis=0,
    )
    heads_here = light_query.shape[1] // HD
    light_q = light_query.reshape(block_count, BLK, heads_here, HD)
    light_k = light_key.reshape(block_count, BLK, heads_here, HD)
    light_v = sparse_out.reshape(block_count, BLK, heads_here, HD)
    rate_blocks = log_decay.reshape(heads_here, block_count, BLK)
    before = passed_along(segments[tokens_here - 1 :] + 1, "seq", 1) - 1
    block_parts = []
    for block_index in range(block_count):
        prior_doc = before[0] if block_index == 0 else seg_blocks[block_index - 1, BLK - 1]
        block_parts.append(
            light_local(
                light_q[block_index],
                light_k[block_index],
                light_v[block_index],
                rate_blocks[:, block_index],
                seg_blocks[block_index],
                prior_doc,
            )
        )
    carried = jnp.zeros((heads_here, HD, HD), jnp.float32)
    passed = jnp.ones((heads_here,), jnp.float32)
    for block_item in block_parts:
        carried = block_item[3][:, None, None] * carried + block_item[2]
        passed = passed * block_item[3]
    entering = carried_in(
        (passed, carried), "seq", chain_link, (jnp.ones_like(passed), jnp.zeros_like(carried))
    )[1]
    outputs = []
    for block_index in range(block_count):
        inside, reach_factor, added_state, carry_factor = block_parts[block_index]
        outside = (
            jnp.einsum(
                "thd,hde->the",
                light_q[block_index].astype(jnp.float32),
                entering,
                precision=lax.Precision.HIGHEST,
            )
            * jnp.transpose(reach_factor)[:, :, None]
        )
        outputs.append(inside + outside)
        entering = carry_factor[:, None, None] * entering + added_state
    mixed_out = jnp.concatenate(outputs, axis=0).reshape(tokens_here, heads_here * HD)
    squares = lax.psum(jnp.sum(mixed_out * mixed_out, axis=1), "head")
    norm_scale = lax.rsqrt(squares / (ASKER_CHANNELS * HD) + norm_eps)
    return (sparse_out, (mixed_out * norm_scale[:, None]).astype(jnp.bfloat16))


def solution(mesh):
    in_specs = (
        P("seq", "head"),
        P("seq", "head"),
        P("seq", "head"),
        P("seq", "head"),
        P("seq", "head"),
        P("head", "seq"),
        P("seq"),
        P("seq", None),
    )
    out_specs = (P("seq", "head"), P("seq", "head"))
    return jax.shard_map(body, mesh=mesh, in_specs=in_specs, out_specs=out_specs, check_vma=False)
```

profile of v0, /device:TPU:0, one launch (start us, length us, event | category | flops | bytes accessed | tf_op | source)
XLA Modules:
  0.0 446.0 jit_solution(10736285755465180232)
XLA Ops:
  7.2 1.0 constant_dynamic-update-slice_fusion.1
  8.2 1.0 constant_dynamic-update-slice_fusion
  10.0 1.4 fusion.81
  12.0 3.3 collective-permute-start
  16.4 23.1 %all-gather.2 = s32[16,1,256]{2,1,0:T(1,128)S(1)} all-gather(s32[1,1,256]{2,1,0:T(1,128)} %bitcast.191), channel_id=1, replica_groups=mesh['seq'=16,'head'=2] {'seq'}, dimensions={0}, use_global_device_ids=true | all-gather | bytes 17408 | tf_op jit(solution)/shard_map/all_gather | solution.py:107
  40.3 1.7 fusion.78
  42.0 1.4 copy.198
  45.7 1.7 fusion.77
  47.4 1.3 copy.201
  48.7 1.3 copy.199
  50.0 1.3 copy.204
  52.4 2.8 fusion.55
  57.3 1.7 compare_convert_fusion.1
  59.7 28.8 %all-gather.6.cloned.1.call-done = bf16[4096,1024]{1,0:T(8,128)(2,1)} async-done(((bf16[256,1024]{1,0:T(8,128)(2,1)}), bf16[4096,1024]{1,0:T(8,128)(2,1)}) %all-gather.6.cloned.1.call-update) | async-done | bytes 8388624 | tf_op jit(solution)/shard_map/all_gather | solution.py:106
  88.4 14.6 %bitcast_convert_fusion = bf16[2,12,128,1024]{3,1,2,0:T(8,128)(2,1)S(1)} fusion(bf16[16,2,128,1024]{3,2,1,0:T(8,128)(2,1)} %bitcast.162, pred[16,2]{0,1:T(4,128)(4,1)S(1)} %iota_compare_fusion.3, pred[2,12,16]{2,1,0:T(8,128)(4,1)S(1)} %iota_compare_fusion.1), kind=kOutput, calls=%fused_computation.13 | convolution fusion | flops 204473088 | bytes 14680480 | tf_op jit(solution)/shard_map/bkpj,pjnc->bknc/dot_general | solution.py:115
  103.1 1.3 fusion.75
  104.4 1.7 copy.145
  106.1 1.7 copy.136
  107.9 2.9 pad_maximum_fusion.2
  110.8 3.7 copy.140
  114.5 14.5 %fusion.85 = f32[4,1664,128,8]{2,1,3,0:T(8,128)} fusion(bf16[1664,4,128,1]{0,2,3,1:T(8,128)(2,1)} %bitcast.165, bf16[128,4,8,128]{0,3,2,1:T(8,128)(2,1)} %bitcast.167), kind=kOutput, calls=%fused_computation.142 | convolution fusion | flops 1744830464 | bytes 30015488 | tf_op jit(solution)/shard_map/qkgd,nkd->kgqn/dot_general | solution.py:46
  129.0 11.3 %fusion.84 = f32[4,8,128]{2,1,0:T(8,128)S(1)} fusion(pred[128,1664]{0,1:T(8,128)(4,1)} %get-tuple-element.160, bf16[1664,4,128,1]{0,2,3,1:T(8,128)(2,1)} %bitcast.166, bf16[128,4,8,128]{0,3,2,1:T(8,128)(2,1)} %bitcast.168), kind=kOutput, calls=%fused_computation.141 | convolution fusion | flops 1772095104 | bytes 2981888 | tf_op jit(solution)/shard_map/sub | solution.py:57
  140.3 3.6 copy.137
  143.9 2.3 copy.147
  146.2 14.6 %fusion.86 = f32[4,1664,128,8]{2,1,3,0:T(8,128)} fusion(bf16[1664,4,128,1]{0,2,3,1:T(8,128)(2,1)} %bitcast.163, bf16[128,4,8,128]{0,3,2,1:T(8,128)(2,1)} %bitcast.169), kind=kOutput, calls=%fused_computation.143 | convolution fusion | flops 1744830464 | bytes 30015488 | tf_op jit(solution)/shard_map/qkgd,nkd->kgqn/dot_general | solution.py:46
  160.8 10.8 %fusion.83 = f32[4,8,128]{2,1,0:T(8,128)S(1)} fusion(pred[128,1664]{0,1:T(8,128)(4,1)} %get-tuple-element.161, bf16[1664,4,128,1]{0,2,3,1:T(8,128)(2,1)S(1)} %bitcast.164, bf16[128,4,8,128]{0,3,2,1:T(8,128)(2,1)} %bitcast.170), kind=kOutput, calls=%fused_computation.140 | convolution fusion | flops 1772095104 | bytes 2981888 | tf_op jit(solution)/shard_map/sub | solution.py:57
  171.6 2.3 copy.146
  174.0 16.0 %fusion.41 = bf16[4,128,8,128]{3,1,2,0:T(8,128)(2,1)} fusion(bf16[1664,4,128,1]{0,2,3,1:T(8,128)(2,1)} %bitcast.186, f32[4,8,128]{2,1,0:T(8,128)S(1)} %fusion.84, f32[4,1664,128,8]{2,1,3,0:T(8,128)} %fusion.85, pred[128,1664]{0,1:T(8,128)(4,1)} %get-tuple-element.160), kind=kOutput, calls=%fused_computation.57 | convolution fusion | flops 1779439232 | bytes 30244864 | tf_op jit(solution)/shard_map/kgqn,nkd->qkgd/dot_general | solution.py:59
  190.0 3.5 fusion.31
  193.5 17.0 %fusion.40 = bf16[4,128,8,128]{3,1,2,0:T(8,128)(2,1)} fusion(bf16[1664,4,128,1]{0,2,3,1:T(8,128)(2,1)} %bitcast.187, f32[4,8,128]{2,1,0:T(8,128)S(1)} %fusion.83, f32[4,1664,128,8]{2,1,3,0:T(8,128)} %fusion.86, pred[128,1664]{0,1:T(8,128)(4,1)} %get-tuple-element.161), kind=kOutput, calls=%fused_computation.56 | convolution fusion | flops 1779439232 | bytes 30244864 | tf_op jit(solution)/shard_map/kgqn,nkd->qkgd/dot_general | solution.py:59
  210.5 4.8 %multiply_add_fusion = f32[32,128,128]{2,1,0:T(8,128)} fusion(f32[32,128,128]{2,1,0:T(8,128)S(1)} %fusion.31, bf16[128,32,128]{0,2,1:T(8,128)(2,1)} %bitcast.182, bf16[128,32,128]{0,2,1:T(8,128)(2,1)S(1)} %bitcast.178, f32[128,32]{0,1:T(8,128)S(1)} %get-tuple-element.159, f32[32]{0:T(128)S(1)} %get-tuple-element.136, f32[32]{0:T(128)S(1)} %exponential_multiply_fusion.1), kind=kOutput, calls=%fused_computation.47 | convolution fusion | flops 807927808 | bytes 6308096 | tf_op jit(solution)/shard_map/shd,she->hde/dot_general | solution.py:79
  215.6 2.7 fusion.76
  218.3 1.3 copy.200
  219.8 1.8 copy.205
  223.1 31.9 %all-reduce = f32[512]{0:T(512)S(1)} all-reduce(f32[512]{0:T(512)S(1)} %dynamic-update-slice), channel_id=2, replica_groups=mesh['seq'=16,'head'=2] {'seq'}, use_global_device_ids=true, to_apply=%add | all-reduce | flops 512 | bytes 4096
  255.0 2.3 copy.152
  257.3 2.3 copy.153
  259.7 4.8 %fusion.42 = f32[32,128,128]{1,2,0:T(8,128)} fusion(bf16[128,32,128]{0,2,1:T(8,128)(2,1)} %bitcast.181, bf16[128,32,128]{0,2,1:T(8,128)(2,1)} %bitcast.173, bf16[128,32,128]{0,2,1:T(8,128)(2,1)} %bitcast.175, f32[32,128]{1,0:T(8,128)S(1)} %copy-done.13, pred[128,128]{1,0:T(8,128)(4,1)S(1)} %copy.158), kind=kOutput, calls=%fused_computation.58 | convolution fusion | flops 271056896 | bytes 5275648 | tf_op jit(solution)/shard_map/hts,shd->thd/dot_general | solution.py:72
  264.4 4.4 fusion.43
  268.8 3.2 pad_maximum_fusion.1
  272.0 110.3 %all-gather.8.cloned.1.call-done = f32[512,128,128]{2,1,0:T(8,128)} async-done(((f32[32,128,128]{2,1,0:T(8,128)}), f32[512,128,128]{2,1,0:T(8,128)}) %all-gather.8.cloned.1.call-update) | async-done | bytes 33554448 | tf_op jit(solution)/shard_map/all_gather | solution.py:21
  382.3 32.0 %while.14 = (s32[]{:T(128)}, f32[32,128,128]{2,1,0:T(8,128)S(1)}, s32[]{:T(128)}, f32[16,32]{1,0:T(8,128)S(1)}, f32[16,32,128,128]{3,2,1,0:T(8,128)}, /*index=5*/s32[]{:T(128)}, s32[]{:T(128)}) while((s32[]{:T(128)}, f32[32,128,128]{2,1,0:T(8,128)S(1)}, s32[]{:T(128)}, f32[16,32]{1,0:T(8,128)S(1)}, ...), condition=%wide.region_9.10_spmd.clone, body=%wide.region_8.9_spmd.clone.sunk | while | flops 2097156 | bytes 6291945 | solution.py:30
  382.3 2.1 fusion.109
  384.4 2.1 fusion.109
  386.6 2.1 fusion.109
  388.7 2.1 fusion.109
  390.8 2.1 fusion.109
  393.0 2.1 fusion.109
  395.1 2.1 fusion.109
  397.2 2.1 fusion.109
  399.4 2.1 fusion.109
  401.5 2.1 fusion.109
  403.6 2.1 fusion.109
  405.8 2.1 fusion.109
  407.9 2.1 fusion.109
  410.1 2.1 fusion.109
  412.2 2.1 fusion.109
  414.3 4.0 fusion.24
  418.3 2.2 fusion.23
  420.6 2.4 multiply_reduce_fusion
  423.0 5.6 %copy.172 = f32[256,32,128]{0,2,1:T(8,128)} copy(f32[256,32,128]{2,0,1:T(8,128)} %get-tuple-element.141) | data formatting | bytes 8388608 | tf_op jit(solution)/shard_map/concatenate | solution.py:181
  428.6 4.9 %psum.7 = f32[256]{0:T(256)S(1)} all-reduce(f32[256]{0:T(256)S(1)} %get-tuple-element.140), channel_id=1, replica_groups=mesh['seq'=16,'head'=2] {'head'}, use_global_device_ids=true, to_apply=%region_11.12 | all-reduce | flops 256 | bytes 2048 | tf_op jit(solution)/shard_map/psum | solution.py:182
  433.5 2.5 fusion.22
  436.0 2.9 copy.173
  (99 shorter events, 7.9 us)
Async XLA Ops:
  7.2 81.2 %all-gather.6.cloned.1.call-start = ((), (), s32[]{:S(2)}) async-start(), calls=%async_computation | async-start | bytes 8912896 | tf_op jit(solution)/shard_map/all_gather | solution.py:106
  9.2 0.8 copy-start.5
  10.0 372.3 %all-gather.8.cloned.1.call-start = ((), (), s32[]{:S(2)}) async-start(), calls=%async_computation.1 | async-start | bytes 35651584 | tf_op jit(solution)/shard_map/all_gather | solution.py:21
  12.0 43.2 %collective-permute-start = (s32[1]{0:T(128)}, s32[1]{0:T(128)}, u32[]{:S(2)}, u32[]{:S(2)}) collective-permute-start(s32[1]{0:T(128)} %add.64), channel_id=1, source_target_pairs={{0,2},{2,4},{4,6},{6,8},{8,10},{10,12},{12,14},{14,16},{16,18},{18... | collective-permute-start | bytes 20 | tf_op jit(solution)/shard_map/ppermute | solution.py:16
  42.0 1.4 copy-start.17
  42.0 3.0 copy-start.16
  45.4 13.6 %copy-start.12 = (f32[32,128]{1,0:T(8,128)}, f32[32,128]{1,0:T(8,128)S(1)}, u32[]{:S(2)}) copy-start(f32[32,128]{1,0:T(8,128)S(1)} %reduce_window_sum.17) | copy-start | bytes 49156
  45.7 13.3 %copy-start.10 = (f32[32,128]{1,0:T(8,128)}, f32[32,128]{1,0:T(8,128)S(1)}, u32[]{:S(2)}) copy-start(f32[32,128]{1,0:T(8,128)S(1)} %reduce_window_sum.18) | copy-start | bytes 49156
  48.7 2.9 copy-start.6
  106.1 1.8 copy-start.8
  106.1 1.8 copy-start.9
  146.2 14.6 %copy-start.2 = (bf16[1664,512]{0,1:T(8,128)(2,1)S(1)}, bf16[1664,512]{0,1:T(8,128)(2,1)}, u32[]{:S(2)}) copy-start(bf16[1664,512]{0,1:T(8,128)(2,1)} %copy.147) | copy-start | bytes 5111812
  174.0 16.0 %copy-start.3 = (bf16[128,4096]{0,1:T(8,128)(2,1)S(1)}, bf16[128,4096]{0,1:T(8,128)(2,1)}, u32[]{:S(2)}) copy-start(bf16[128,4096]{0,1:T(8,128)(2,1)} %copy.201) | copy-start | bytes 3145732
  193.5 17.0 %copy-start = (f32[32,128,128]{2,1,0:T(8,128)}, f32[32,128,128]{2,1,0:T(8,128)S(1)}, u32[]{:S(2)}) copy-start(f32[32,128,128]{2,1,0:T(8,128)S(1)} %fusion.31) | copy-start | bytes 6291460
  193.5 17.0 %copy-start.4 = (bf16[128,4096]{0,1:T(8,128)(2,1)S(1)}, bf16[128,4096]{0,1:T(8,128)(2,1)}, u32[]{:S(2)}) copy-start(bf16[128,4096]{0,1:T(8,128)(2,1)} %copy.204) | copy-start | bytes 3145732
  218.3 3.2 copy-start.19
  255.0 4.6 %copy-start.13 = (f32[32,128]{1,0:T(8,128)S(1)}, f32[32,128]{1,0:T(8,128)}, u32[]{:S(2)}) copy-start(f32[32,128]{1,0:T(8,128)} %copy-done.12) | copy-start | bytes 49156
  259.7 4.8 %copy-start.11 = (f32[32,128]{1,0:T(8,128)S(1)}, f32[32,128]{1,0:T(8,128)}, u32[]{:S(2)}) copy-start(f32[32,128]{1,0:T(8,128)} %copy-done.10) | copy-start | bytes 49156
  382.3 32.0 %copy-start.15 = (f32[128,32]{0,1:T(8,128)S(1)}, f32[128,32]{0,1:T(8,128)}, u32[]{:S(2)}) copy-start(f32[128,32]{0,1:T(8,128)} %get-tuple-element.185) | copy-start | bytes 49156
  414.3 4.0 copy-start.1
  414.3 4.0 copy-start.7
  414.3 4.0 copy-start.14
  414.3 4.0 copy-start.18
Sparse Core Ops, SparseCore 0:
  10.7 77.6 all-gather.5
  215.5 166.7 all-gather.7
where the time goes:
time: 450 us; the launch traced here: 446 us
  waiting for transfers between devices  139 us (31%)
  matrix products  122 us (27%)
  blocking collectives  59.9 us (13%)
  local copies, waits for them, and re-layouts  51.5 us (11%)
  other arithmetic  50.9 us (11%)
  between operations  18.4 us (4%)
    all_gather x1, waiting for transfers between devices, carried_in(): pieces = jax.tree.map(lambda part: lax.all_gather(part, axis), value)  110 us
    dot_general x2, matrix products, attend_block(): jnp.einsum('kgqn,nkd->qkgd', weights, value_part, preferred_element_type=...  33 us
    unnamed x1, blocking collectives  31.9 us
    select_n x15, other arithmetic, turn(): jnp.where(position < mine, new, old)  31.4 us
    dot_general x2, matrix products, attend_block(): jnp.einsum('qkgd,nkd->kgqn', queries, key_part, preferred_element_type=jn...  29 us
    all_gather x1, waiting for transfers between devices, body(): kv_portion = lax.all_gather(kv_local, 'seq', axis=0, tiled=True)  28.8 us
    all_gather x1, blocking collectives, body(): seg_portion = lax.all_gather(segments, 'seq', axis=0, tiled=True)  23.1 us
    sub x2, matrix products, attend_block(): lifted = jnp.exp(scores - highest)  22.1 us
  transfers between devices with their start and end apart: 3, of which 2 were waited for; matrix products, arithmetic and copies ran while one was open for 10% of the time, Pallas kernels for 0%

commit v1 on v0

--- a/solution.py
+++ b/solution.py
@@ -103,7 +103,16 @@
     wanted = jnp.max(jnp.where(owner_match, inner_index[None, :], -1), axis=1)
     wanted_safe = jnp.clip(wanted, 0, block_count - 1)
     owner_table = owner_index.reshape(block_count, block_list.shape[1])
-    kv_portion = lax.all_gather(kv_local, "seq", axis=0, tiled=True)
+    ways = lax.axis_size("seq")
+    up = [(d, (d + 1) % ways) for d in range(ways)]
+    down = [(d, (d - 1) % ways) for d in range(ways)]
+    earlier_2, later = ([kv_local], [kv_local])
+    for _ in range(ways // 2):
+        earlier_2.append(lax.ppermute(earlier_2[-1], "seq", up))
+    for _ in range((ways - 1) // 2):
+        later.append(lax.ppermute(later[-1], "seq", down))
+    line = jnp.concatenate([*earlier_2[::-1], *later[1:]], axis=0)
+    kv_portion = jnp.roll(line, (lax.axis_index("seq") - ways // 2) * kv_local.shape[0], axis=0)
     seg_portion = lax.all_gather(segments, "seq", axis=0, tiled=True)
     portion_shards = kv_portion.shape[0] // tokens_here
     kv_view = kv_portion.reshape(portion_shards, block_count, BLK, 2 * kv_width)

time: 450 us -> 550 us (1.22)
  local copies, waits for them, and re-layouts: 51.5 us -> 105 us
  starting transfers between devices: 3.38 us -> 56.2 us
  waiting for transfers between devices: 139 us -> 121 us
  blocking collectives: 59.9 us -> 68.8 us
    ppermute x0 -> x15, starting transfers between devices: none -> 53.9 us  [the longest x8 38.2 us: body(): earlier_2.append(lax.ppermute(earlier_2[-1], 'seq', up))]
    unnamed x51 -> x102, local copies, waits for them, and re-layouts: 13.9 us -> 56.6 us
    all_gather x1 -> x0, waiting for transfers between devices: 28.8 us -> none  [body(): kv_portion = lax.all_gather(kv_local, 'seq', axis=0, tiled=True)]
    unnamed x1, blocking collectives: 31.9 us -> 41.4 us
    ppermute x0 -> x15, waiting for transfers between devices: none -> 8.44 us  [the longest x8 6.37 us: body(): earlier_2.append(lax.ppermute(earlier_2[-1], 'seq', up))]
    dynamic_slice x0 -> x1, local copies, waits for them, and re-layouts: none -> 7.61 us  [body(): jnp.roll(line, (lax.axis_index('seq') - ways // 2) * kv_local.shape[0], a...]
  transfers between devices with their start and end apart: 3 -> 17, of which waited for: 2 -> 6; matrix products, arithmetic and copies ran while one was open for 10% -> 12% of each run, Pallas kernels for 0% -> 0%
where the time goes in v1:
time: 550 us; the launch traced here: 544 us
  matrix products  123 us (22%)
  waiting for transfers between devices  121 us (22%)
  local copies, waits for them, and re-layouts  105 us (19%)
  blocking collectives  68.8 us (13%)
  starting transfers between devices  56.2 us (10%)
  other arithmetic  50.6 us (9%)
  between operations  18.8 us (3%)
    all_gather x1, waiting for transfers between devices, carried_in(): pieces = jax.tree.map(lambda part: lax.all_gather(part, axis), value)  112 us
    unnamed x102, local copies, waits for them, and re-layouts  56.6 us
    unnamed x1, blocking collectives  41.4 us
    ppermute x8, starting transfers between devices, body(): earlier_2.append(lax.ppermute(earlier_2[-1], 'seq', up))  38.2 us
    dot_general x2, matrix products, attend_block(): jnp.einsum('kgqn,nkd->qkgd', weights, value_part, preferred_element_type=...  33 us
    select_n x15, other arithmetic, turn(): jnp.where(position < mine, new, old)  31.4 us
    dot_general x2, matrix products, attend_block(): jnp.einsum('qkgd,nkd->kgqn', queries, key_part, preferred_element_type=jn...  29.1 us
    all_gather x1, blocking collectives, body(): seg_portion = lax.all_gather(segments, 'seq', axis=0, tiled=True)  22.5 us
  transfers between devices with their start and end apart: 17, of which 6 were waited for; matrix products, arithmetic and copies ran while one was open for 12% of the time, Pallas kernels for 0%

profile of v1, /device:TPU:0, one launch (start us, length us, event | category | flops | bytes accessed | tf_op | source)
XLA Modules:
  0.0 543.7 jit_solution(15432757342246992777)
XLA Ops:
  11.0 5.0 collective-permute-start.8
  18.1 2.2 collective-permute-start.15
  20.3 2.7 fusion.78
  25.0 5.4 collective-permute-start.1
  30.5 6.1 %collective-permute-done.1 = bf16[256,1024]{1,0:T(8,128)(2,1)} collective-permute-done((bf16[256,1024]{1,0:T(8,128)(2,1)}, bf16[256,1024]{1,0:T(8,128)(2,1)}, u32[]{:S(2)}, u32[]{:S(2)}) %collective-permute-start.1) | collective-permute-done | bytes 524320 | tf_op jit(solution)/shard_map/ppermute | solution.py:111
  36.9 2.3 copy.198
  39.3 22.5 %all-gather.2 = s32[16,1,256]{2,1,0:T(1,128)S(1)} all-gather(s32[1,1,256]{2,1,0:T(1,128)S(1)} %bitcast.191), channel_id=1, replica_groups=mesh['seq'=16,'head'=2] {'seq'}, dimensions={0}, use_global_device_ids=true | all-gather | bytes 17408 | tf_op jit(solution)/shard_map/all_gather | solution.py:116
  69.3 4.3 collective-permute-start.10
  73.7 4.8 collective-permute-start.4
  78.5 2.1 collective-permute-done.10
  80.6 4.6 collective-permute-start.11
  85.3 7.1 %collective-permute-start.5 = (bf16[256,1024]{1,0:T(8,128)(2,1)S(1)}, bf16[256,1024]{1,0:T(8,128)(2,1)S(1)}, u32[]{:S(2)}, u32[]{:S(2)}) collective-permute-start(bf16[256,1024]{1,0:T(8,128)(2,1)S(1)} %collective-permute-done.4), channel_id=1, source_target_pairs={{0,2},{2,4},{4,6},{6,8},{8,10},{10,12},{12,14},{14,16},{16,18},{18... | collective-permute-start | bytes 1572872 | tf_op jit(solution)/shard_map/ppermute | solution.py:111
  92.4 2.6 fusion.55
  96.7 9.8 %collective-permute-start.6 = (bf16[256,1024]{1,0:T(8,128)(2,1)S(1)}, bf16[256,1024]{1,0:T(8,128)(2,1)}, u32[]{:S(2)}, u32[]{:S(2)}) collective-permute-start(bf16[256,1024]{1,0:T(8,128)(2,1)S(1)} %collective-permute-done.5), channel_id=1, source_target_pairs={{0,2},{2,4},{4,6},{6,8},{8,10},{10,12},{12,14},{14,16},{16,18},{18... | collective-permute-start | bytes 1572872 | tf_op jit(solution)/shard_map/ppermute | solution.py:111
  110.9 9.8 %collective-permute-start.7 = (bf16[256,1024]{1,0:T(8,128)(2,1)}, bf16[256,1024]{1,0:T(8,128)(2,1)S(1)}, u32[]{:S(2)}, u32[]{:S(2)}) collective-permute-start(bf16[256,1024]{1,0:T(8,128)(2,1)} %collective-permute-done.6), channel_id=1, source_target_pairs={{0,2},{2,4},{4,6},{6,8},{8,10},{10,12},{12,14},{14,16},{16,18},{18... | collective-permute-start | bytes 1572872 | tf_op jit(solution)/shard_map/ppermute | solution.py:111
  121.3 2.0 compare_convert_fusion.1
  149.9 1.9 constant_dynamic-update-slice_fusion.13
  155.6 1.9 constant_dynamic-update-slice_fusion.10
  166.9 7.6 %constant_dynamic-slice_fusion = bf16[4096,1024]{1,0:T(8,128)(2,1)} fusion(bf16[8192,1024]{1,0:T(8,128)(2,1)} %constant_dynamic-update-slice_fusion.2, s32[]{:T(128)S(6)} %select_n.77), kind=kLoop, calls=%fused_computation.156 | loop fusion | bytes 16777220 | tf_op jit(solution)/shard_map/jit(_roll_dynamic)/dynamic_slice | solution.py:115
  174.5 14.8 %bitcast_convert_fusion = bf16[2,12,128,1024]{3,1,2,0:T(8,128)(2,1)S(1)} fusion(bf16[16,2,128,1024]{3,2,1,0:T(8,128)(2,1)} %bitcast.160, pred[16,2]{0,1:T(4,128)(4,1)S(1)} %iota_compare_fusion.3, pred[2,12,16]{2,1,0:T(8,128)(4,1)S(1)} %iota_compare_fusion.1), kind=kOutput, calls=%fused_computation.13 | convolution fusion | flops 204473088 | bytes 14680480 | tf_op jit(solution)/shard_map/bkpj,pjnc->bknc/dot_general | solution.py:124
  194.0 2.9 pad_maximum_fusion.2
  196.9 3.7 copy.140
  200.6 14.5 %fusion.85 = f32[4,1664,128,8]{2,1,3,0:T(8,128)} fusion(bf16[1664,4,128,1]{0,2,3,1:T(8,128)(2,1)} %bitcast.165, bf16[128,4,8,128]{0,3,2,1:T(8,128)(2,1)} %bitcast.167), kind=kOutput, calls=%fused_computation.177 | convolution fusion | flops 1744830464 | bytes 30015488 | tf_op jit(solution)/shard_map/qkgd,nkd->kgqn/dot_general | solution.py:46
  215.1 11.3 %fusion.84 = f32[4,8,128]{2,1,0:T(8,128)S(1)} fusion(pred[128,1664]{0,1:T(8,128)(4,1)} %get-tuple-element.160, bf16[1664,4,128,1]{0,2,3,1:T(8,128)(2,1)} %bitcast.166, bf16[128,4,8,128]{0,3,2,1:T(8,128)(2,1)} %bitcast.168), kind=kOutput, calls=%fused_computation.176 | convolution fusion | flops 1772095104 | bytes 2981888 | tf_op jit(solution)/shard_map/sub | solution.py:57
  226.4 3.6 copy.137
  230.0 2.3 copy.147
  232.3 14.6 %fusion.86 = f32[4,1664,128,8]{2,1,3,0:T(8,128)} fusion(bf16[1664,4,128,1]{0,2,3,1:T(8,128)(2,1)} %bitcast.163, bf16[128,4,8,128]{0,3,2,1:T(8,128)(2,1)} %bitcast.169), kind=kOutput, calls=%fused_computation.178 | convolution fusion | flops 1744830464 | bytes 30015488 | tf_op jit(solution)/shard_map/qkgd,nkd->kgqn/dot_general | solution.py:46
  246.9 10.8 %fusion.83 = f32[4,8,128]{2,1,0:T(8,128)S(1)} fusion(pred[128,1664]{0,1:T(8,128)(4,1)} %get-tuple-element.161, bf16[1664,4,128,1]{0,2,3,1:T(8,128)(2,1)S(1)} %bitcast.164, bf16[128,4,8,128]{0,3,2,1:T(8,128)(2,1)} %bitcast.170), kind=kOutput, calls=%fused_computation.175 | convolution fusion | flops 1772095104 | bytes 2981888 | tf_op jit(solution)/shard_map/sub | solution.py:57
  257.7 2.3 copy.146
  260.1 16.0 %fusion.41 = bf16[4,128,8,128]{3,1,2,0:T(8,128)(2,1)} fusion(bf16[1664,4,128,1]{0,2,3,1:T(8,128)(2,1)} %bitcast.186, f32[4,8,128]{2,1,0:T(8,128)S(1)} %fusion.84, f32[4,1664,128,8]{2,1,3,0:T(8,128)} %fusion.85, pred[128,1664]{0,1:T(8,128)(4,1)} %get-tuple-element.160), kind=kOutput, calls=%fused_computation.57 | convolution fusion | flops 1779439232 | bytes 30244864 | tf_op jit(solution)/shard_map/kgqn,nkd->qkgd/dot_general | solution.py:59
  276.1 3.5 fusion.31
  279.7 17.0 %fusion.40 = bf16[4,128,8,128]{3,1,2,0:T(8,128)(2,1)} fusion(bf16[1664,4,128,1]{0,2,3,1:T(8,128)(2,1)} %bitcast.187, f32[4,8,128]{2,1,0:T(8,128)S(1)} %fusion.83, f32[4,1664,128,8]{2,1,3,0:T(8,128)} %fusion.86, pred[128,1664]{0,1:T(8,128)(4,1)} %get-tuple-element.161), kind=kOutput, calls=%fused_computation.56 | convolution fusion | flops 1779439232 | bytes 30244864 | tf_op jit(solution)/shard_map/kgqn,nkd->qkgd/dot_general | solution.py:59
  296.7 4.8 multiply_add_fusion
  301.8 2.7 fusion.76
  309.1 41.4 %all-reduce = f32[512]{0:T(512)S(1)} all-reduce(f32[512]{0:T(512)S(1)} %dynamic-update-slice), channel_id=2, replica_groups=mesh['seq'=16,'head'=2] {'seq'}, use_global_device_ids=true, to_apply=%add | all-reduce | flops 512 | bytes 4096
  350.5 2.3 copy.152
  352.8 2.3 copy.153
  355.1 4.9 fusion.42
  360.0 4.5 fusion.43
  364.6 3.1 pad_maximum_fusion.1
  367.7 112.2 %all-gather.5.cloned.1.call-done = f32[512,128,128]{2,1,0:T(8,128)} async-done(((f32[32,128,128]{2,1,0:T(8,128)}), f32[512,128,128]{2,1,0:T(8,128)}) %all-gather.5.cloned.1.call-update) | async-done | bytes 33554448 | tf_op jit(solution)/shard_map/all_gather | solution.py:21
  479.9 32.0 %while.14 = (s32[]{:T(128)}, f32[32,128,128]{2,1,0:T(8,128)S(1)}, s32[]{:T(128)}, f32[16,32]{1,0:T(8,128)S(1)}, f32[16,32,128,128]{3,2,1,0:T(8,128)}, /*index=5*/s32[]{:T(128)}, s32[]{:T(128)}) while((s32[]{:T(128)}, f32[32,128,128]{2,1,0:T(8,128)S(1)}, s32[]{:T(128)}, f32[16,32]{1,0:T(8,128)S(1)}, ...), condition=%wide.region_9.10_spmd.clone, body=%wide.region_8.9_spmd.clone.sunk | while | flops 2097156 | bytes 6291945 | solution.py:30
  479.9 2.1 fusion.109
  482.0 2.1 fusion.109
  484.2 2.1 fusion.109
  486.3 2.1 fusion.109
  488.4 2.1 fusion.109
  490.6 2.1 fusion.109
  492.7 2.1 fusion.109
  494.8 2.1 fusion.109
  497.0 2.1 fusion.109
  499.1 2.1 fusion.109
  501.2 2.1 fusion.109
  503.4 2.1 fusion.109
  505.5 2.1 fusion.109
  507.6 2.1 fusion.109
  509.8 2.1 fusion.109
  511.9 4.0 fusion.24
  515.9 2.2 fusion.23
  518.2 2.4 multiply_reduce_fusion
  520.6 5.7 %copy.172 = f32[256,32,128]{0,2,1:T(8,128)} copy(f32[256,32,128]{2,0,1:T(8,128)} %get-tuple-element.141) | data formatting | bytes 8388608 | tf_op jit(solution)/shard_map/concatenate | solution.py:190
  526.2 4.9 psum.7
  531.2 2.5 fusion.22
  533.7 2.9 copy.173
  (179 shorter events, 67.9 us)
Async XLA Ops:
  7.2 32.1 %copy-start.18 = (s32[256]{0:T(256)S(1)}, s32[256]{0:T(256)}, u32[]{:S(2)}) copy-start(s32[256]{0:T(256)} %param.16) | copy-start | bytes 3076
  7.2 17.5 %copy-start.25 = (s32[2,12]{1,0:T(2,128)S(1)}, s32[2,12]{1,0:T(2,128)}, u32[]{:S(2)}) copy-start(s32[2,12]{1,0:T(2,128)} %param.17) | copy-start | bytes 292
  7.2 57.3 %copy-start.17 = (f32[32,256]{1,0:T(8,128)S(1)}, f32[32,256]{1,0:T(8,128)}, u32[]{:S(2)}) copy-start(f32[32,256]{1,0:T(8,128)} %param.15) | copy-start | bytes 98308
  7.2 472.7 %all-gather.5.cloned.1.call-start = ((), (), s32[]{:S(2)}) async-start(), calls=%async_computation | async-start | bytes 35651584 | tf_op jit(solution)/shard_map/all_gather | solution.py:21
  10.6 14.4 %collective-permute-start = (bf16[256,1024]{1,0:T(8,128)(2,1)}, bf16[256,1024]{1,0:T(8,128)(2,1)}, u32[]{:S(2)}, u32[]{:S(2)}) collective-permute-start(bf16[256,1024]{1,0:T(8,128)(2,1)} %constant_dynamic-update-slice_fusion), channel_id=1, source_target_pairs={{0,2},{2,4},{4,6},{6,8},{8,10},{10,12},{12,14},{14,16},{16,18},{18... | collective-permute-start | bytes 1572872 | tf_op jit(solution)/shard_map/ppermute | solution.py:111
  11.0 50.8 %collective-permute-start.8 = (bf16[256,1024]{1,0:T(8,128)(2,1)}, bf16[256,1024]{1,0:T(8,128)(2,1)}, u32[]{:S(2)}, u32[]{:S(2)}) collective-permute-start(bf16[256,1024]{1,0:T(8,128)(2,1)} %constant_dynamic-update-slice_fusion), channel_id=1, source_target_pairs={{0,30},{2,0},{4,2},{6,4},{8,6},{10,8},{12,10},{14,12},{16,14},{18,... | collective-permute-start | bytes 1572872 | tf_op jit(solution)/shard_map/ppermute | solution.py:113
  18.1 90.3 %collective-permute-start.15 = (s32[1]{0:T(128)}, s32[1]{0:T(128)}, u32[]{:S(2)}, u32[]{:S(2)}) collective-permute-start(s32[1]{0:T(128)} %add.77), channel_id=1, source_target_pairs={{0,2},{2,4},{4,6},{6,8},{8,10},{10,12},{12,14},{14,16},{16,18},{18... | collective-permute-start | bytes 20 | tf_op jit(solution)/shard_map/ppermute | solution.py:16
  25.0 11.7 %collective-permute-start.1 = (bf16[256,1024]{1,0:T(8,128)(2,1)}, bf16[256,1024]{1,0:T(8,128)(2,1)}, u32[]{:S(2)}, u32[]{:S(2)}) collective-permute-start(bf16[256,1024]{1,0:T(8,128)(2,1)} %collective-permute-done), channel_id=1, source_target_pairs={{0,2},{2,4},{4,6},{6,8},{8,10},{10,12},{12,14},{14,16},{16,18},{18... | collective-permute-start | bytes 1572872 | tf_op jit(solution)/shard_map/ppermute | solution.py:111
  36.7 25.2 %collective-permute-start.2 = (bf16[256,1024]{1,0:T(8,128)(2,1)}, bf16[256,1024]{1,0:T(8,128)(2,1)}, u32[]{:S(2)}, u32[]{:S(2)}) collective-permute-start(bf16[256,1024]{1,0:T(8,128)(2,1)} %collective-permute-done.1), channel_id=1, source_target_pairs={{0,2},{2,4},{4,6},{6,8},{8,10},{10,12},{12,14},{14,16},{16,18},{18... | collective-permute-start | bytes 1572872 | tf_op jit(solution)/shard_map/ppermute | solution.py:111
  61.8 7.4 %collective-permute-start.9 = (bf16[256,1024]{1,0:T(8,128)(2,1)}, bf16[256,1024]{1,0:T(8,128)(2,1)}, u32[]{:S(2)}, u32[]{:S(2)}) collective-permute-start(bf16[256,1024]{1,0:T(8,128)(2,1)} %collective-permute-done.8), channel_id=1, source_target_pairs={{0,30},{2,0},{4,2},{6,4},{8,6},{10,8},{12,10},{14,12},{16,14},{18,... | collective-permute-start | bytes 1572872 | tf_op jit(solution)/shard_map/ppermute | solution.py:113
  61.9 11.8 %collective-permute-start.3 = (bf16[256,1024]{1,0:T(8,128)(2,1)}, bf16[256,1024]{1,0:T(8,128)(2,1)}, u32[]{:S(2)}, u32[]{:S(2)}) collective-permute-start(bf16[256,1024]{1,0:T(8,128)(2,1)} %collective-permute-done.2), channel_id=1, source_target_pairs={{0,2},{2,4},{4,6},{6,8},{8,10},{10,12},{12,14},{14,16},{16,18},{18... | collective-permute-start | bytes 1572872 | tf_op jit(solution)/shard_map/ppermute | solution.py:111
  64.8 67.4 %copy-start.12 = (f32[32,128]{1,0:T(8,128)}, f32[32,128]{1,0:T(8,128)S(1)}, u32[]{:S(2)}) copy-start(f32[32,128]{1,0:T(8,128)S(1)} %reduce_window_sum.17) | copy-start | bytes 49156
  65.1 67.2 %copy-start.10 = (f32[32,128]{1,0:T(8,128)}, f32[32,128]{1,0:T(8,128)S(1)}, u32[]{:S(2)}) copy-start(f32[32,128]{1,0:T(8,128)S(1)} %reduce_window_sum.18) | copy-start | bytes 49156
  66.4 69.6 %copy-start.5 = (bf16[256,512]{1,0:T(8,128)(2,1)S(1)}, bf16[256,512]{1,0:T(8,128)(2,1)}, u32[]{:S(2)}) copy-start(bf16[256,512]{1,0:T(8,128)(2,1)} %param.11) | copy-start | bytes 786436
  67.7 69.0 %copy-start.6 = (bf16[256,512]{1,0:T(8,128)(2,1)S(1)}, bf16[256,512]{1,0:T(8,128)(2,1)}, u32[]{:S(2)}) copy-start(bf16[256,512]{1,0:T(8,128)(2,1)} %param.12) | copy-start | bytes 786436
  69.3 11.3 %collective-permute-start.10 = (bf16[256,1024]{1,0:T(8,128)(2,1)}, bf16[256,1024]{1,0:T(8,128)(2,1)S(1)}, u32[]{:S(2)}, u32[]{:S(2)}) collective-permute-start(bf16[256,1024]{1,0:T(8,128)(2,1)} %collective-permute-done.9), channel_id=1, source_target_pairs={{0,30},{2,0},{4,2},{6,4},{8,6},{10,8},{12,10},{14,12},{16,14},{18,... | collective-permute-start | bytes 1572872 | tf_op jit(solution)/shard_map/ppermute | solution.py:113
  73.7 11.6 %collective-permute-start.4 = (bf16[256,1024]{1,0:T(8,128)(2,1)}, bf16[256,1024]{1,0:T(8,128)(2,1)S(1)}, u32[]{:S(2)}, u32[]{:S(2)}) collective-permute-start(bf16[256,1024]{1,0:T(8,128)(2,1)} %collective-permute-done.3), channel_id=1, source_target_pairs={{0,2},{2,4},{4,6},{6,8},{8,10},{10,12},{12,14},{14,16},{16,18},{18... | collective-permute-start | bytes 1572872 | tf_op jit(solution)/shard_map/ppermute | solution.py:111
  78.5 63.6 %copy-start.19 = (s32[128]{0:T(128)}, s32[128]{0:T(128)S(1)}, u32[]{:S(2)}) copy-start(s32[128]{0:T(128)S(1)} %get-tuple-element.170) | copy-start | bytes 1540
  78.5 63.6 %copy-start.21 = (s32[128]{0:T(128)}, s32[128]{0:T(128)S(1)}, u32[]{:S(2)}) copy-start(s32[128]{0:T(128)S(1)} %get-tuple-element.171) | copy-start | bytes 1540
  80.6 14.5 %collective-permute-start.11 = (bf16[256,1024]{1,0:T(8,128)(2,1)S(1)}, bf16[256,1024]{1,0:T(8,128)(2,1)S(1)}, u32[]{:S(2)}, u32[]{:S(2)}) collective-permute-start(bf16[256,1024]{1,0:T(8,128)(2,1)S(1)} %collective-permute-done.10), channel_id=1, source_target_pairs={{0,30},{2,0},{4,2},{6,4},{8,6},{10,8},{12,10},{14,12},{16,14},{18,... | collective-permute-start | bytes 1572872 | tf_op jit(solution)/shard_map/ppermute | solution.py:113
  85.3 11.4 %collective-permute-start.5 = (bf16[256,1024]{1,0:T(8,128)(2,1)S(1)}, bf16[256,1024]{1,0:T(8,128)(2,1)S(1)}, u32[]{:S(2)}, u32[]{:S(2)}) collective-permute-start(bf16[256,1024]{1,0:T(8,128)(2,1)S(1)} %collective-permute-done.4), channel_id=1, source_target_pairs={{0,2},{2,4},{4,6},{6,8},{8,10},{10,12},{12,14},{14,16},{16,18},{18... | collective-permute-start | bytes 1572872 | tf_op jit(solution)/shard_map/ppermute | solution.py:111
  95.1 15.8 %collective-permute-start.12 = (bf16[256,1024]{1,0:T(8,128)(2,1)S(1)}, bf16[256,1024]{1,0:T(8,128)(2,1)S(1)}, u32[]{:S(2)}, u32[]{:S(2)}) collective-permute-start(bf16[256,1024]{1,0:T(8,128)(2,1)S(1)} %collective-permute-done.11), channel_id=1, source_target_pairs={{0,30},{2,0},{4,2},{6,4},{8,6},{10,8},{12,10},{14,12},{16,14},{18,... | collective-permute-start | bytes 1572872 | tf_op jit(solution)/shard_map/ppermute | solution.py:113
  96.7 14.2 %collective-permute-start.6 = (bf16[256,1024]{1,0:T(8,128)(2,1)S(1)}, bf16[256,1024]{1,0:T(8,128)(2,1)}, u32[]{:S(2)}, u32[]{:S(2)}) collective-permute-start(bf16[256,1024]{1,0:T(8,128)(2,1)S(1)} %collective-permute-done.5), channel_id=1, source_target_pairs={{0,2},{2,4},{4,6},{6,8},{8,10},{10,12},{12,14},{14,16},{16,18},{18... | collective-permute-start | bytes 1572872 | tf_op jit(solution)/shard_map/ppermute | solution.py:111
  110.9 13.0 %collective-permute-start.13 = (bf16[256,1024]{1,0:T(8,128)(2,1)S(1)}, bf16[256,1024]{1,0:T(8,128)(2,1)S(1)}, u32[]{:S(2)}, u32[]{:S(2)}) collective-permute-start(bf16[256,1024]{1,0:T(8,128)(2,1)S(1)} %collective-permute-done.12), channel_id=1, source_target_pairs={{0,30},{2,0},{4,2},{6,4},{8,6},{10,8},{12,10},{14,12},{16,14},{18,... | collective-permute-start | bytes 1572872 | tf_op jit(solution)/shard_map/ppermute | solution.py:113
  110.9 13.2 %collective-permute-start.7 = (bf16[256,1024]{1,0:T(8,128)(2,1)}, bf16[256,1024]{1,0:T(8,128)(2,1)S(1)}, u32[]{:S(2)}, u32[]{:S(2)}) collective-permute-start(bf16[256,1024]{1,0:T(8,128)(2,1)} %collective-permute-done.6), channel_id=1, source_target_pairs={{0,2},{2,4},{4,6},{6,8},{8,10},{10,12},{12,14},{14,16},{16,18},{18... | collective-permute-start | bytes 1572872 | tf_op jit(solution)/shard_map/ppermute | solution.py:111
  123.9 20.6 %collective-permute-start.14 = (bf16[256,1024]{1,0:T(8,128)(2,1)S(1)}, bf16[256,1024]{1,0:T(8,128)(2,1)S(1)}, u32[]{:S(2)}, u32[]{:S(2)}) collective-permute-start(bf16[256,1024]{1,0:T(8,128)(2,1)S(1)} %collective-permute-done.13), channel_id=1, source_target_pairs={{0,30},{2,0},{4,2},{6,4},{8,6},{10,8},{12,10},{14,12},{16,14},{18,... | collective-permute-start | bytes 1572872 | tf_op jit(solution)/shard_map/ppermute | solution.py:113
  190.5 3.5 copy-start.8
  190.5 3.5 copy-start.9
  232.3 14.6 %copy-start.2 = (bf16[1664,512]{0,1:T(8,128)(2,1)S(1)}, bf16[1664,512]{0,1:T(8,128)(2,1)}, u32[]{:S(2)}) copy-start(bf16[1664,512]{0,1:T(8,128)(2,1)} %copy.147) | copy-start | bytes 5111812
  260.1 16.0 %copy-start.3 = (bf16[128,4096]{0,1:T(8,128)(2,1)S(1)}, bf16[128,4096]{0,1:T(8,128)(2,1)}, u32[]{:S(2)}) copy-start(bf16[128,4096]{0,1:T(8,128)(2,1)} %copy.201) | copy-start | bytes 3145732
  279.6 17.0 %copy-start = (f32[32,128,128]{2,1,0:T(8,128)}, f32[32,128,128]{2,1,0:T(8,128)S(1)}, u32[]{:S(2)}) copy-start(f32[32,128,128]{2,1,0:T(8,128)S(1)} %fusion.31) | copy-start | bytes 6291460
  279.6 17.0 %copy-start.4 = (bf16[128,4096]{0,1:T(8,128)(2,1)S(1)}, bf16[128,4096]{0,1:T(8,128)(2,1)}, u32[]{:S(2)}) copy-start(bf16[128,4096]{0,1:T(8,128)(2,1)} %copy.204) | copy-start | bytes 3145732
  279.6 17.0 %copy-start.16 = (f32[128,32]{0,1:T(8,128)S(1)}, f32[128,32]{0,1:T(8,128)}, u32[]{:S(2)}) copy-start(f32[128,32]{0,1:T(8,128)} %get-tuple-element.159) | copy-start | bytes 49156
  279.6 17.0 %copy-start.24 = (f32[32]{0:T(128)S(1)}, f32[32]{0:T(128)}, u32[]{:S(2)}) copy-start(f32[32]{0:T(128)} %get-tuple-element.136) | copy-start | bytes 388
  279.7 17.0 %copy-start.27 = (f32[32]{0:T(128)S(1)}, f32[32]{0:T(128)}, u32[]{:S(2)}) copy-start(f32[32]{0:T(128)} %exponential_multiply_fusion.1) | copy-start | bytes 388
  296.6 5.0 copy-start.20
  296.6 5.0 copy-start.22
  301.5 6.1 %copy-start.28 = (u32[32]{0:T(128)S(1)}, u32[32]{0:T(128)}, u32[]{:S(2)}) copy-start(u32[32]{0:T(128)} %constant.111) | copy-start | bytes 388
  301.5 7.3 %copy-start.26 = (f32[32]{0:T(128)S(1)}, f32[32]{0:T(128)}, u32[]{:S(2)}) copy-start(f32[32]{0:T(128)} %get-tuple-element.124) | copy-start | bytes 388
  301.5 53.6 %copy-start.13 = (f32[32,128]{1,0:T(8,128)S(1)}, f32[32,128]{1,0:T(8,128)}, u32[]{:S(2)}) copy-start(f32[32,128]{1,0:T(8,128)} %copy-done.12) | copy-start | bytes 49156
  304.5 55.5 %copy-start.11 = (f32[32,128]{1,0:T(8,128)S(1)}, f32[32,128]{1,0:T(8,128)}, u32[]{:S(2)}) copy-start(f32[32,128]{1,0:T(8,128)} %copy-done.10) | copy-start | bytes 49156
  479.9 32.0 %copy-start.15 = (f32[128,32]{0,1:T(8,128)S(1)}, f32[128,32]{0,1:T(8,128)}, u32[]{:S(2)}) copy-start(f32[128,32]{0,1:T(8,128)} %get-tuple-element.185) | copy-start | bytes 49156
  511.9 4.0 copy-start.1
  511.9 4.0 copy-start.7
  511.9 4.0 copy-start.14
  511.9 4.0 copy-start.23
Sparse Core Ops, SparseCore 0:
  301.7 178.1 all-gather.4
